TPU v7x, 32 devices: a whole 2x2x4 slice. The times are simulated.
32 devices in a mesh: row: 8 (over z, core), col: 4 (over y, x).
Axes of the slice: x: 2, y: 2, z: 4, core: 2. Of those that a mesh axis runs over, the one named last changes fastest.
Arguments:
- diag_tile: float32 [128, 128], P('row'), may hold values from -20 to 100, as said below
- panel: bfloat16 [16384, 128], P(('row', 'col')), may hold values from -1.796875 to 1.796875
- trailing: float32 [16384, 2048], P('row', 'col'), may hold values from -6 to 6
Outputs:
- solved: bfloat16 [16384, 128], P(('row', 'col'))
- updated: float32 [16384, 2048], P('row', 'col')
Inputs may be any that keep to these rules, and one draw needn't show every extreme that they name: diag_tile is symmetric and positive definite, with its smallest eigenvalue 1 or more.
All inputs are finite; a program needn't handle non-finite values.
Results may differ from a plain program's by a relative error of at most 0.0051.
Values may be sent and summed in bfloat16 or wider, within the bound.
No kernel may reach another device: no remote copies, remote signals or barrier semaphores. Data moves between devices by JAX's collectives and lax.ppermute only.
A program may use at most 64 MiB of HBM per device.

v0:
```python
import jax
import jax.numpy as jnp
from jax import lax
from jax.sharding import PartitionSpec as P


def from_root(value, axis, source):
    kept = jnp.where(lax.axis_index(axis) == source, value, 0).astype(value.dtype)
    return lax.psum(kept, axis)


def per_device(diag_tile, panel, trailing):
    whole_tile = lax.all_gather(diag_tile, "row", axis=0, tiled=True)
    factor = jnp.linalg.cholesky(whole_tile)
    identity = jnp.eye(whole_tile.shape[0], dtype=whole_tile.dtype)
    inverse = lax.linalg.triangular_solve(factor, identity, left_side=True, lower=True).astype(
        jnp.bfloat16
    )
    solved_rows = lax.dot_general(
        panel, inverse, (((1,), (1,)), ((), ())), preferred_element_type=jnp.float32
    ).astype(jnp.bfloat16)
    row_panel = lax.all_gather(solved_rows, "col", axis=0, tiled=True)
    rows_dev = row_panel.shape[0]
    cols_dev = trailing.shape[1]
    col_start = lax.axis_index("col") * cols_dev
    source_row = col_start // rows_dev
    offset = col_start % rows_dev
    picked = lax.dynamic_slice_in_dim(row_panel, offset, cols_dev, 0)
    col_panel = from_root(picked, "row", source_row)
    update = lax.dot_general(
        row_panel, col_panel, (((1,), (1,)), ((), ())), preferred_element_type=jnp.float32
    )
    row_ids = lax.axis_index("row") * rows_dev + jnp.arange(rows_dev, dtype=jnp.int32)
    col_ids = col_start + jnp.arange(cols_dev, dtype=jnp.int32)
    lower_part = row_ids[:, None] >= col_ids[None, :]
    updated = jnp.where(lower_part, trailing - update, trailing)
    return (solved_rows, updated)


def solution(mesh):
    in_specs = (P("row", None), P(("row", "col"), None), P("row", "col"))
    out_specs = (P(("row", "col"), None), P("row", "col"))
    return jax.shard_map(
        per_device, mesh=mesh, in_specs=in_specs, out_specs=out_specs, check_vma=False
    )
```

profile of v0, /device:TPU:0, one launch (start us, length us, event | category | flops | bytes accessed | tf_op | source)
XLA Modules:
  0.0 123.7 jit_solution(9039450617726350077)
XLA Ops:
  7.2 0.0 copy-start
  7.2 0.0 all-reduce.2.cloned.1.call-start
  7.2 15.9 %all_gather.6 = f32[128,128]{1,0:T(8,128)S(1)} all-gather(f32[16,128]{1,0:T(8,128)} %param.3), channel_id=1, replica_groups=mesh['row'=8,'col'=4] {'row'}, dimensions={0}, use_global_device_ids=true | all-gather | bytes 73728 | tf_op jit(solution)/shard_map/all_gather | solution.py:13
  23.2 0.1 copy.8
  23.3 11.7 %cholesky.17 = f32[128,128]{1,0:T(8,128)S(1)} custom-call(f32[128,128]{1,0:T(8,128)S(1)} %fusion.3), custom_call_target="Cholesky" | custom-call | tf_op jit(solution)/shard_map/jit(cholesky)/cholesky | solution.py:14
  35.0 0.6 compare_reduce_fusion
  35.7 0.7 fusion.1
  36.3 9.8 %custom-call.6 = f32[1,128,128]{1,2,0:T(8,128)S(1)} custom-call(f32[1,128,128]{2,1,0:T(8,128)S(1)} %fusion.1), custom_call_target="InvertDiagBlocksLowerTriangular" | custom-call | tf_op jit(solution)/shard_map/triangular_solve | solution.py:16
  46.1 0.3 convolution_convert_fusion.1
  46.4 0.0 copy-done
  46.4 0.2 fusion
  46.6 10.3 %all_gather.7 = bf16[2048,128]{0,1:T(8,128)(2,1)S(1)} all-gather(bf16[512,128]{0,1:T(8,128)(2,1)S(1)} %fusion), channel_id=1, replica_groups=mesh['row'=8,'col'=4] {'col'}, dimensions={0}, use_global_device_ids=true | all-gather | bytes 655360 | tf_op jit(solution)/shard_map/all_gather | solution.py:22
  56.9 0.7 dynamic-slice_select_fusion
  57.6 0.0 all-reduce.2.cloned.1.call-update
  57.6 0.8 copy.9
  58.4 54.4 %all-reduce.2.cloned.1.call-done = bf16[512,128]{0,1:T(8,128)(2,1)} async-done(((bf16[512,128]{0,1:T(8,128)(2,1)}), bf16[512,128]{0,1:T(8,128)(2,1)}) %all-reduce.2.cloned.1.call-update) | async-done | bytes 131088 | tf_op jit(solution)/shard_map/psum | solution.py:9
  112.8 4.1 %subtract_select_fusion = f32[2048,512]{1,0:T(8,128)} fusion(f32[2048,512]{1,0:T(8,128)} %param.5, bf16[2048,128]{0,1:T(8,128)(2,1)S(1)} %all_gather.7, bf16[512,128]{0,1:T(8,128)(2,1)} %all-reduce.2.cloned.1.call-done, s32[512]{0:T(512)S(1)} %iota_add_fusion.1, s32[2048]{0:T(1024)S(1)} %iota_add_fusion), kind=kOutput, calls=%fused_computation | convolution fusion | flops 271581184 | bytes 9054208 | tf_op jit(solution)/shard_map/dot_general | solution.py:30
  (4 shorter events, 0.1 us)
Async XLA Ops:
  7.2 39.2 %copy-start = (bf16[512,128]{1,0:T(8,128)(2,1)S(1)}, bf16[512,128]{1,0:T(8,128)(2,1)}, u32[]{:S(2)}) copy-start(bf16[512,128]{1,0:T(8,128)(2,1)} %param.4) | copy-start | bytes 393220
  7.2 105.6 %all-reduce.2.cloned.1.call-start = ((), (), s32[]{:S(2)}) async-start(), calls=%async_computation | async-start | bytes 262144 | tf_op jit(solution)/shard_map/psum | solution.py:9
Sparse Core Ops, SparseCore 0:
  57.7 55.0 all-reduce.1
where the time goes:
time: 124 us
  waiting for transfers between devices  54.4 us (44%)
  blocking collectives  26.2 us (21%)
  other arithmetic  23.6 us (19%)
  between operations  14.1 us (11%)
  matrix products  4.52 us (4%)
    psum x1, waiting for transfers between devices, from_root(): return lax.psum(kept, axis)  54.4 us
    all_gather x1, blocking collectives, per_device(): whole_tile = lax.all_gather(diag_tile, 'row', axis=0, tiled=True)  15.9 us
    another operation x3, other arithmetic, per_device(): factor = jnp.linalg.cholesky(whole_tile)  12.4 us
    another operation x2, other arithmetic, per_device(): lax.linalg.triangular_solve(factor, identity, left_side=True, lower=True)  10.5 us
    all_gather x1, blocking collectives, per_device(): row_panel = lax.all_gather(solved_rows, 'col', axis=0, tiled=True)  10.3 us
    dot_general x1, matrix products, per_device(): lax.dot_general(row_panel, col_panel, (((1,), (1,)), ((), ())), preferred...  4.08 us
  transfers between devices with their start and end apart: 1, of which 1 were waited for; matrix products, arithmetic and copies ran while one was open for 1% of the time, Pallas kernels for 0%

commit v1 on v0

--- a/solution.py
+++ b/solution.py
@@ -2,11 +2,12 @@
 import jax.numpy as jnp
 from jax import lax
 from jax.sharding import PartitionSpec as P
+from jax.lax import all_gather
 
 
 def from_root(value, axis, source):
     kept = jnp.where(lax.axis_index(axis) == source, value, 0).astype(value.dtype)
-    return lax.psum(kept, axis)
+    return jnp.sum(all_gather(kept, axis), axis=0)
 
 
 def per_device(diag_tile, panel, trailing):

time: 124 us -> 93.6 us (0.75)
  waiting for transfers between devices: 54.4 us -> 21.7 us
  local copies, waits for them, and re-layouts: 0.86 us -> 2.48 us
    psum x1 -> x0, waiting for transfers between devices: 54.4 us -> none  [from_root(): return lax.psum(kept, axis)]
    all_gather x0 -> x1, waiting for transfers between devices: none -> 21.7 us  [from_root(): return jnp.sum(all_gather(kept, axis), axis=0)]
    unnamed x3 -> x4, local copies, waits for them, and re-layouts: 0.77 us -> 2.39 us
where the time goes in v1:
time: 93.6 us; the launch traced here: 93.4 us
  blocking collectives  26.2 us (28%)
  other arithmetic  24.3 us (26%)
  waiting for transfers between devices  21.7 us (23%)
  between operations  14.1 us (15%)
  matrix products  4.53 us (5%)
  local copies, waits for them, and re-layouts  2.48 us (3%)
    all_gather x1, waiting for transfers between devices, from_root(): return jnp.sum(all_gather(kept, axis), axis=0)  21.7 us
    all_gather x1, blocking collectives, per_device(): whole_tile = lax.all_gather(diag_tile, 'row', axis=0, tiled=True)  15.9 us
    another operation x3, other arithmetic, per_device(): factor = jnp.linalg.cholesky(whole_tile)  12.4 us
    another operation x2, other arithmetic, per_device(): lax.linalg.triangular_solve(factor, identity, left_side=True, lower=True)  10.5 us
    all_gather x1, blocking collectives, per_device(): row_panel = lax.all_gather(solved_rows, 'col', axis=0, tiled=True)  10.3 us
    dot_general x1, matrix products, per_device(): lax.dot_general(row_panel, col_panel, (((1,), (1,)), ((), ())), preferred...  4.08 us
    unnamed x4, local copies, waits for them, and re-layouts  2.39 us
  transfers between devices with their start and end apart: 1, of which 1 were waited for; matrix products, arithmetic and copies ran while one was open for 1% of the time, Pallas kernels for 0%

profile of v1, /device:TPU:0, one launch (start us, length us, event | category | flops | bytes accessed | tf_op | source)
XLA Modules:
  0.0 93.4 jit_solution(12331205428901651391)
XLA Ops:
  7.2 0.0 copy-start
  7.2 0.0 all-gather.3.cloned.1.call-start
  7.2 15.9 %all_gather.12 = f32[128,128]{1,0:T(8,128)S(1)} all-gather(f32[16,128]{1,0:T(8,128)} %param.3), channel_id=1, replica_groups=mesh['row'=8,'col'=4] {'row'}, dimensions={0}, use_global_device_ids=true | all-gather | bytes 73728 | tf_op jit(solution)/shard_map/all_gather | solution.py:14
  23.2 0.1 copy.8
  23.3 11.7 %cholesky.17 = f32[128,128]{1,0:T(8,128)S(1)} custom-call(f32[128,128]{1,0:T(8,128)S(1)} %fusion.3), custom_call_target="Cholesky" | custom-call | tf_op jit(solution)/shard_map/jit(cholesky)/cholesky | solution.py:15
  35.0 0.6 compare_reduce_fusion
  35.7 0.7 fusion.1
  36.3 9.8 %custom-call.6 = f32[1,128,128]{1,2,0:T(8,128)S(1)} custom-call(f32[1,128,128]{2,1,0:T(8,128)S(1)} %fusion.1), custom_call_target="InvertDiagBlocksLowerTriangular" | custom-call | tf_op jit(solution)/shard_map/triangular_solve | solution.py:17
  46.1 0.3 convolution_convert_fusion.1
  46.4 0.0 copy-done
  46.4 0.2 fusion
  46.6 10.3 %all_gather.13 = bf16[2048,128]{0,1:T(8,128)(2,1)S(1)} all-gather(bf16[512,128]{0,1:T(8,128)(2,1)S(1)} %fusion), channel_id=1, replica_groups=mesh['row'=8,'col'=4] {'col'}, dimensions={0}, use_global_device_ids=true | all-gather | bytes 655360 | tf_op jit(solution)/shard_map/all_gather | solution.py:23
  56.9 0.7 dynamic-slice_select_fusion
  57.6 0.0 all-gather.3.cloned.1.call-update
  57.6 0.8 copy.9
  58.4 21.7 %all-gather.3.cloned.1.call-done = bf16[4096,128]{0,1:T(8,128)(2,1)} async-done(((bf16[512,128]{0,1:T(8,128)(2,1)}), bf16[4096,128]{0,1:T(8,128)(2,1)}) %all-gather.3.cloned.1.call-update) | async-done | bytes 1048592 | tf_op jit(solution)/shard_map/all_gather | solution.py:10
  80.1 1.6 %copy.10 = bf16[16,8,8,512]{3,2,1,0:T(8,128)(2,1)S(1)} copy(bf16[16,8,8,512]{3,1,2,0:T(8,128)(2,1)} %bitcast.20) | data formatting | bytes 2097152
  81.7 0.8 bitcast_reduce_fusion
  82.5 4.1 %subtract_select_fusion = f32[2048,512]{1,0:T(8,128)} fusion(f32[2048,512]{1,0:T(8,128)} %param.5, bf16[2048,128]{0,1:T(8,128)(2,1)S(1)} %all_gather.13, bf16[512,128]{0,1:T(8,128)(2,1)S(1)} %bitcast_reduce_fusion, s32[512]{0:T(512)S(1)} %iota_add_fusion.1, s32[2048]{0:T(1024)S(1)} %iota_add_fusion), kind=kOutput, calls=%fused_computation | convolution fusion | flops 271581184 | bytes 9054208 | tf_op jit(solution)/shard_map/dot_general | solution.py:31
  (4 shorter events, 0.1 us)
Async XLA Ops:
  7.2 39.2 %copy-start = (bf16[512,128]{1,0:T(8,128)(2,1)S(1)}, bf16[512,128]{1,0:T(8,128)(2,1)}, u32[]{:S(2)}) copy-start(bf16[512,128]{1,0:T(8,128)(2,1)} %param.4) | copy-start | bytes 393220
  7.2 72.9 %all-gather.3.cloned.1.call-start = ((), (), s32[]{:S(2)}) async-start(), calls=%async_computation | async-start | bytes 1179648 | tf_op jit(solution)/shard_map/all_gather | solution.py:10
Sparse Core Ops, SparseCore 0:
  57.7 22.2 all-gather.2
